TPU v7x, 512 devices: a whole 4x4x16 slice. The times are simulated.
512 devices in a mesh: tm: 16 (over y, x_lo, core), expert: 32 (over x_hi, z).
Axes of the slice: x: 4 (x_hi: 2, x_lo: 2; x = x_hi * 2 + x_lo), y: 4, z: 16, core: 2. Of those that a mesh axis runs over, the one named last changes fastest.
Arguments:
- latents: bfloat16 [32, 2048, 1024], P('expert', 'tm'), may hold values from -16 to 16
- queries: bfloat16 [32, 2048, 1024], P('expert', 'tm'), may hold values from -6 to 6
- keys: bfloat16 [32, 2048, 1024], P('expert', 'tm'), may hold values from -6 to 6
- values: bfloat16 [32, 2048, 1024], P('expert', 'tm'), may hold values from -8 to 8
- inpaint_mask: int32 [32, 2048], P('expert', 'tm'), may hold values 0 or 1
- key_bias: bfloat16 [16], replicated, may hold values from -3 to 3
- out_weight: bfloat16 [1024, 1024], replicated, may hold values from -0.1875 to 0.1875
- modulation: float32 [32, 2, 1024], P('expert'), may hold values from -3 to 3
- branch_gates: float32 [32, 2, 1024], P('expert'), may hold values from 0.5 to 1.5
- expert_ids: int32 [32, 2048, 2], P('expert', 'tm'), may hold values from 0 to 31, as said below
- gate_values: float32 [32, 2048, 2], P('expert', 'tm'), may hold values from 0.2 to 1
- up_weight: bfloat16 [32, 1024, 1024], P('expert', None, 'tm'), may hold values from -0.1875 to 0.1875
- down_weight: bfloat16 [32, 1024, 1024], P('expert', 'tm'), may hold values from -0.1875 to 0.1875
Outputs:
- layer_out: bfloat16 [32, 2048, 1024], P('expert', 'tm')
Inputs may be any that keep to these rules, and one draw needn't show every extreme that they name: `expert_ids`: A token's two ids differ. Within each device's block of 128 positions of one clip, no id is named more than 16 times, and one id is named exactly 16 times; that id is the same for all clips at the same block position.
All inputs are finite; a program needn't handle non-finite values. No bound on the sum of `inpaint_mask` on one device may be relied on, other than what follows from the above.
Results may differ from a plain program's by a relative error of at most 0.01.
Values may be sent and summed in bfloat16 or wider, within the bound.
A program may use at most 128 MiB of HBM per device.

v0:
```python
import jax
import jax.numpy as jnp
from jax import lax
from jax.sharding import PartitionSpec as P

eps = 1e-06
query_block = 512


def head_attention(query_rows, key_rows, value_rows, offset_row):
    outputs = []
    for first in range(0, query_rows.shape[0], query_block):
        block = query_rows[first : first + query_block]
        scores = (
            jnp.dot(block, key_rows.T, preferred_element_type=jnp.float32) + offset_row[None, :]
        )
        highest = jnp.max(scores, axis=1, keepdims=True)
        unscaled = jnp.exp(scores - highest)
        total = jnp.sum(unscaled, axis=1, keepdims=True)
        weighted = jnp.dot(
            unscaled.astype(jnp.bfloat16), value_rows, preferred_element_type=jnp.float32
        )
        outputs.append((weighted / total).astype(jnp.bfloat16))
    return jnp.concatenate(outputs, axis=0)


def layer_norm(mixed, shift_row, scale_row):
    center = jnp.mean(mixed, axis=-1, keepdims=True)
    deviation = mixed - center
    variance = jnp.mean(deviation * deviation, axis=-1, keepdims=True)
    return deviation * lax.rsqrt(variance + eps) * (1.0 + scale_row) + shift_row


def on_device(
    latents,
    queries,
    keys,
    values,
    inpaint_mask,
    key_bias,
    out_weight,
    modulation,
    branch_gates,
    expert_ids,
    gate_values,
    up_weight,
    down_weight,
):
    tok_rows = latents.shape[1]
    model_width = latents.shape[2]
    head_count = key_bias.shape[0]
    head_width = model_width // head_count
    score_scale = head_width ** (-0.5)
    full_up, full_down = (
        lax.all_gather(up_weight, "tm", axis=2, tiled=True),
        lax.all_gather(down_weight, "tm", axis=1, tiled=True),
    )
    scaled_queries = queries[0] * jnp.asarray(score_scale, jnp.bfloat16)
    offsets = jnp.where(
        inpaint_mask[0][:, None] == 1, key_bias[None, :], jnp.zeros((), jnp.bfloat16)
    )
    offset_cols = (
        jnp.zeros((tok_rows, head_count, head_width), jnp.bfloat16).at[:, :, 0].set(offsets)
    )
    packed = jnp.concatenate(
        [
            scaled_queries.reshape(tok_rows, head_count, head_width),
            keys[0].reshape(tok_rows, head_count, head_width),
            values[0].reshape(tok_rows, head_count, head_width),
            offset_cols,
        ],
        axis=2,
    )
    packed = jnp.transpose(packed, (1, 0, 2))
    gathered = lax.all_to_all(packed, "tm", split_axis=0, concat_axis=0, tiled=True)
    clip_rows = gathered.reshape(-1, 4 * head_width)
    head_out = head_attention(
        clip_rows[:, :head_width],
        clip_rows[:, head_width : 2 * head_width],
        clip_rows[:, 2 * head_width : 3 * head_width],
        clip_rows[:, 3 * head_width].astype(jnp.float32),
    )
    head_out = head_out.reshape(head_count, tok_rows, head_width)
    attended_heads = lax.all_to_all(head_out, "tm", split_axis=0, concat_axis=0, tiled=True)
    projected = jnp.einsum(
        "hid,hdo->io",
        attended_heads,
        out_weight.reshape(head_count, head_width, model_width),
        preferred_element_type=jnp.float32,
    )
    mixed = latents[0].astype(jnp.float32) + branch_gates[0, 0][None, :] * projected
    normed = layer_norm(mixed, modulation[0, 0][None, :], modulation[0, 1][None, :]).astype(
        jnp.bfloat16
    )
    local_experts = up_weight.shape[0]
    source_count = lax.axis_size("expert")
    expert_count = local_experts * source_count
    capacity = 4 * tok_rows // expert_count
    choice_list = expert_ids[0].reshape(2 * tok_rows)
    hits = (choice_list[:, None] == jnp.arange(expert_count, dtype=jnp.int32)[None, :]).astype(
        jnp.int32
    )
    ranks = jnp.sum((jnp.cumsum(hits, axis=0) - 1) * hits, axis=1)
    target = ranks * expert_count + choice_list
    placing = (
        jnp.arange(capacity * expert_count, dtype=jnp.int32)[:, None] == target[None, :]
    ).astype(jnp.bfloat16)
    doubled = jnp.repeat(normed, 2, axis=0)
    slots = jnp.dot(placing, doubled, preferred_element_type=jnp.float32).astype(jnp.bfloat16)
    slots = slots.reshape(capacity, expert_count, model_width)
    arrived = lax.all_to_all(slots, "expert", split_axis=1, concat_axis=1, tiled=True)
    slot_count = arrived.shape[0]
    grouped = arrived.reshape(slot_count, source_count, local_experts, model_width)
    hidden = jax.nn.gelu(
        jnp.einsum("csed,edf->csef", grouped, full_up, preferred_element_type=jnp.float32),
        approximate=True,
    ).astype(jnp.bfloat16)
    produced = jnp.einsum(
        "csef,efd->csed", hidden, full_down, preferred_element_type=jnp.float32
    ).astype(jnp.bfloat16)
    produced = produced.reshape(slot_count, source_count * local_experts, model_width)
    returned = lax.all_to_all(produced, "expert", split_axis=1, concat_axis=1, tiled=True)
    picked = jnp.einsum(
        "sa,sd->ad",
        placing,
        returned.reshape(capacity * expert_count, model_width),
        preferred_element_type=jnp.float32,
    )
    picked = picked.reshape(tok_rows, 2, model_width)
    combined = jnp.sum(gate_values[0][:, :, None] * picked, axis=1)
    layer_out = (mixed + branch_gates[0, 1][None, :] * combined).astype(jnp.bfloat16)
    return layer_out[None]


def solution(mesh):
    placed = (
        P("expert", "tm", None),
        P("expert", "tm", None),
        P("expert", "tm", None),
        P("expert", "tm", None),
        P("expert", "tm"),
        P(),
        P(),
        P("expert", None, None),
        P("expert", None, None),
        P("expert", "tm", None),
        P("expert", "tm", None),
        P("expert", None, "tm"),
        P("expert", "tm", None),
    )
    return jax.shard_map(
        on_device, mesh=mesh, in_specs=placed, out_specs=P("expert", "tm", None), check_vma=False
    )
```

profile of v0, /device:TPU:32, one launch (start us, length us, event | category | flops | bytes accessed | tf_op | source)
XLA Modules:
  0.0 219.5 jit_solution(16701565516031589247)
XLA Ops:
  6.5 1.3 copy.26
  7.8 1.1 copy.27
  9.0 1.1 copy.28
  11.5 1.1 fusion.65
  12.6 5.6 %all-to-all-start = ((bf16[16,128,256]{1,2,0:T(8,128)(2,1)}), bf16[16,128,256]{1,2,0:T(8,128)(2,1)}, u32[]{:S(2)}, u32[]{:S(2)}) async-start(bf16[16,128,256]{1,2,0:T(8,128)(2,1)} %fusion.65), calls=%async_computation | async-start | bytes 2097152 | tf_op jit(solution)/shard_map/all_to_all | solution.py:75
  20.3 14.5 %all-to-all-done = bf16[16,128,256]{1,2,0:T(8,128)(2,1)} async-done(((bf16[16,128,256]{1,2,0:T(8,128)(2,1)}), bf16[16,128,256]{1,2,0:T(8,128)(2,1)}, u32[]{:S(2)}, u32[]{:S(2)}) %all-to-all-start) | async-done | bytes 1048608 | tf_op jit(solution)/shard_map/all_to_all | solution.py:75
  34.8 1.5 copy.29
  39.2 2.1 fusion
  42.2 2.5 %fusion.2 = (f32[512]{0:T(512)S(1)}, f32[512]{0:T(512)S(1)}, f32[512]{0:T(512)S(1)}) fusion(f32[512,2048]{1,0:T(8,128)S(1)} %get-tuple-element.30, f32[512]{0:T(512)S(1)} %get-tuple-element.18, f32[2048]{0:T(1024)S(1)} %convert_reduce_fusion, f32[512]{0:T(512)S(1)} %get-tuple-element.19, f32[512,2048]{1,0:T(8,128)S(1)} %fusion.78, ...), kind=kLoop, calls=%fused_computation.10 | loop fusion | flops 9435648 | bytes 12603392 | tf_op jit(solution)/shard_map/reduce_sum | solution.py:19
  44.7 1.0 fusion.49
  45.7 1.0 fusion.55
  48.4 3.7 %all-to-all-start.1 = ((bf16[16,128,64]{1,2,0:T(8,128)(2,1)}), bf16[16,128,64]{1,2,0:T(8,128)(2,1)S(1)}, u32[]{:S(2)}, u32[]{:S(2)}) async-start(bf16[16,128,64]{1,2,0:T(8,128)(2,1)} %copy_bitcast_fusion), calls=%async_computation.1 | async-start | bytes 524288 | tf_op jit(solution)/shard_map/all_to_all | solution.py:84
  52.2 9.1 %all-to-all-done.1 = bf16[16,128,64]{1,2,0:T(8,128)(2,1)S(1)} async-done(((bf16[16,128,64]{1,2,0:T(8,128)(2,1)}), bf16[16,128,64]{1,2,0:T(8,128)(2,1)S(1)}, u32[]{:S(2)}, u32[]{:S(2)}) %all-to-all-start.1) | async-done | bytes 262176 | tf_op jit(solution)/shard_map/all_to_all | solution.py:84
  62.5 1.0 reshape.208
  63.5 1.5 convolution_convert_fusion
  65.0 1.6 copy.34
  66.6 17.5 %all-to-all-start.2 = ((bf16[16,32,1024]{2,0,1:T(8,128)(2,1)}), bf16[16,32,1024]{2,0,1:T(8,128)(2,1)}, u32[]{:S(2)}, u32[]{:S(2)}) async-start(bf16[16,32,1024]{2,0,1:T(8,128)(2,1)} %copy.34), calls=%async_computation.2 | async-start | bytes 2097152 | tf_op jit(solution)/shard_map/all_to_all | solution.py:111
  84.8 43.0 %all-gather.5.cloned.1.call-done = bf16[1,1024,1024]{2,1,0:T(8,128)(2,1)} async-done(((bf16[1,64,1024]{2,1,0:T(8,128)(2,1)}), bf16[1,1024,1024]{2,1,0:T(8,128)(2,1)}) %all-gather.5.cloned.1.call-update) | async-done | bytes 2097168 | tf_op jit(solution)/shard_map/all_gather | solution.py:56
  127.8 12.3 %all-to-all-done.2 = bf16[16,32,1024]{2,0,1:T(8,128)(2,1)} async-done(((bf16[16,32,1024]{2,0,1:T(8,128)(2,1)}), bf16[16,32,1024]{2,0,1:T(8,128)(2,1)}, u32[]{:S(2)}, u32[]{:S(2)}) %all-to-all-start.2) | async-done | bytes 1048608 | tf_op jit(solution)/shard_map/all_to_all | solution.py:111
  140.1 6.2 %fusion.31 = bf16[16,32,1024]{2,1,0:T(8,128)(2,1)} fusion(bf16[1,1024,1024]{2,1,0:T(8,128)(2,1)} %all-gather.5.cloned.1.call-done, bf16[1,1024,1024]{1,2,0:T(8,128)(2,1)} %all-gather.3.cloned.1.call-done, bf16[16,32,1024]{2,0,1:T(8,128)(2,1)} %all-to-all-done.2), kind=kOutput, calls=%fused_computation.35 | convolution fusion | flops 2152726528 | bytes 6291456 | tf_op jit(solution)/shard_map/csef,efd->csed/dot_general | solution.py:118
  146.3 2.8 %copy.37 = bf16[16,32,1024]{2,0,1:T(8,128)(2,1)} copy(bf16[16,32,1024]{2,1,0:T(8,128)(2,1)} %fusion.31) | data formatting | bytes 2097152 | tf_op jit(solution)/shard_map/convert_element_type | solution.py:120
  149.1 4.5 %all-to-all-start.3 = ((bf16[16,32,1024]{2,0,1:T(8,128)(2,1)}), bf16[16,32,1024]{2,0,1:T(8,128)(2,1)}, u32[]{:S(2)}, u32[]{:S(2)}) async-start(bf16[16,32,1024]{2,0,1:T(8,128)(2,1)} %copy.37), calls=%async_computation.3 | async-start | bytes 2097152 | tf_op jit(solution)/shard_map/all_to_all | solution.py:122
  154.0 55.7 %all-to-all-done.3 = bf16[16,32,1024]{2,0,1:T(8,128)(2,1)} async-done(((bf16[16,32,1024]{2,0,1:T(8,128)(2,1)}), bf16[16,32,1024]{2,0,1:T(8,128)(2,1)}, u32[]{:S(2)}, u32[]{:S(2)}) %all-to-all-start.3) | async-done | bytes 1048608 | tf_op jit(solution)/shard_map/all_to_all | solution.py:122
  209.7 1.8 copy.38
  (49 shorter events, 12.5 us)
Async XLA Ops:
  6.5 54.7 %copy-start = (bf16[1024,1024]{1,0:T(8,128)(2,1)S(1)}, bf16[1024,1024]{1,0:T(8,128)(2,1)}, u32[]{:S(2)}) copy-start(bf16[1024,1024]{1,0:T(8,128)(2,1)} %param.21) | copy-start | bytes 6291460
  6.5 12.4 %copy-start.4 = (s32[1,128,2]{1,2,0:T(2,128)S(1)}, s32[1,128,2]{1,2,0:T(2,128)}, u32[]{:S(2)}) copy-start(s32[1,128,2]{1,2,0:T(2,128)} %param.24) | copy-start | bytes 3076
  6.5 13.7 %copy-start.2 = (f32[1,2,1024]{2,1,0:T(2,128)S(1)}, f32[1,2,1024]{2,1,0:T(2,128)}, u32[]{:S(2)}) copy-start(f32[1,2,1024]{2,1,0:T(2,128)} %param.23) | copy-start | bytes 24580
  12.6 22.2 %all-to-all-start = ((bf16[16,128,256]{1,2,0:T(8,128)(2,1)}), bf16[16,128,256]{1,2,0:T(8,128)(2,1)}, u32[]{:S(2)}, u32[]{:S(2)}) async-start(bf16[16,128,256]{1,2,0:T(8,128)(2,1)} %fusion.65), calls=%async_computation | async-start | bytes 2097152 | tf_op jit(solution)/shard_map/all_to_all | solution.py:75
  18.2 66.6 %all-gather.3.cloned.1.call-start = ((), (), s32[]{:S(2)}) async-start(), calls=%async_computation.4 | async-start | bytes 2228224 | tf_op jit(solution)/shard_map/all_gather | solution.py:55
  46.6 5.5 %copy-start.3 = (f32[1,2,1024]{2,1,0:T(2,128)S(1)}, f32[1,2,1024]{2,1,0:T(2,128)}, u32[]{:S(2)}) copy-start(f32[1,2,1024]{2,1,0:T(2,128)} %param.22) | copy-start | bytes 24580
  46.6 14.6 %copy-start.1 = (bf16[1,128,1024]{2,1,0:T(8,128)(2,1)S(1)}, bf16[1,128,1024]{2,1,0:T(8,128)(2,1)}, u32[]{:S(2)}) copy-start(bf16[1,128,1024]{2,1,0:T(8,128)(2,1)} %param.15) | copy-start | bytes 786436
  48.4 12.9 %all-to-all-start.1 = ((bf16[16,128,64]{1,2,0:T(8,128)(2,1)}), bf16[16,128,64]{1,2,0:T(8,128)(2,1)S(1)}, u32[]{:S(2)}, u32[]{:S(2)}) async-start(bf16[16,128,64]{1,2,0:T(8,128)(2,1)} %copy_bitcast_fusion), calls=%async_computation.1 | async-start | bytes 524288 | tf_op jit(solution)/shard_map/all_to_all | solution.py:84
  66.6 73.5 %all-to-all-start.2 = ((bf16[16,32,1024]{2,0,1:T(8,128)(2,1)}), bf16[16,32,1024]{2,0,1:T(8,128)(2,1)}, u32[]{:S(2)}, u32[]{:S(2)}) async-start(bf16[16,32,1024]{2,0,1:T(8,128)(2,1)} %copy.34), calls=%async_computation.2 | async-start | bytes 2097152 | tf_op jit(solution)/shard_map/all_to_all | solution.py:111
  84.0 43.8 %all-gather.5.cloned.1.call-start = ((), (), s32[]{:S(2)}) async-start(), calls=%async_computation.5 | async-start | bytes 2228224 | tf_op jit(solution)/shard_map/all_gather | solution.py:56
  146.3 65.1 %copy-start.5 = (f32[1,128,2]{1,2,0:T(2,128)S(1)}, f32[1,128,2]{1,2,0:T(2,128)}, u32[]{:S(2)}) copy-start(f32[1,128,2]{1,2,0:T(2,128)} %param.25) | copy-start | bytes 3076
  149.1 60.5 %all-to-all-start.3 = ((bf16[16,32,1024]{2,0,1:T(8,128)(2,1)}), bf16[16,32,1024]{2,0,1:T(8,128)(2,1)}, u32[]{:S(2)}, u32[]{:S(2)}) async-start(bf16[16,32,1024]{2,0,1:T(8,128)(2,1)} %copy.37), calls=%async_computation.3 | async-start | bytes 2097152 | tf_op jit(solution)/shard_map/all_to_all | solution.py:122
Sparse Core Ops, SparseCore 0:
  21.2 47.8 all-gather.2
  87.0 40.7 all-gather.4
where the time goes:
time: 220 us
  waiting for transfers between devices  136 us (62%)
  starting transfers between devices  31.3 us (14%)
  matrix products  17 us (8%)
  between operations  13.7 us (6%)
  local copies, waits for them, and re-layouts  13.2 us (6%)
  other arithmetic  8.24 us (4%)
    all_to_all x1, waiting for transfers between devices, on_device(): lax.all_to_all(produced, 'expert', split_axis=1, concat_axis=1, tiled=True)  55.7 us
    all_gather x1, waiting for transfers between devices, on_device(): lax.all_gather(down_weight, 'tm', axis=1, tiled=True)  43 us
    all_to_all x1, starting transfers between devices, on_device(): lax.all_to_all(slots, 'expert', split_axis=1, concat_axis=1, tiled=True)  17.5 us
    all_to_all x1, waiting for transfers between devices, on_device(): lax.all_to_all(packed, 'tm', split_axis=0, concat_axis=0, tiled=True)  14.5 us
    all_to_all x1, waiting for transfers between devices, on_device(): lax.all_to_all(slots, 'expert', split_axis=1, concat_axis=1, tiled=True)  12.3 us
    all_to_all x1, waiting for transfers between devices, on_device(): lax.all_to_all(head_out, 'tm', split_axis=0, concat_axis=0, tiled=True)  9.1 us
    dot_general x1, matrix products, on_device(): jnp.einsum('csef,efd->csed', hidden, full_down, preferred_element_type=jn...  6.21 us
    all_to_all x1, starting transfers between devices, on_device(): lax.all_to_all(packed, 'tm', split_axis=0, concat_axis=0, tiled=True)  5.55 us
  transfers between devices with their start and end apart: 6, of which 5 were waited for; matrix products, arithmetic and copies ran while one was open for 9% of the time, Pallas kernels for 0%

commit v1 on v0

--- a/solution.py
+++ b/solution.py
@@ -1,3 +1,4 @@
+import functools
 import jax
 import jax.numpy as jnp
 from jax import lax
@@ -5,6 +6,16 @@
 
 eps = 1e-06
 query_block = 512
+
+
+def layers_all_point(own_rows, device_axis):
+    part_next = jnp.stack([own_rows] * lax.psum(1, axis_name=device_axis))
+    return jnp.concatenate(
+        lax.all_to_all(part_next, concat_axis=0, split_axis=0, axis_name=device_axis), axis=1
+    )
+
+
+define_things = functools.partial(layers_all_point, device_axis="tm")
 
 
 def head_attention(query_rows, key_rows, value_rows, offset_row):
@@ -53,7 +64,7 @@
     score_scale = head_width ** (-0.5)
     full_up, full_down = (
         lax.all_gather(up_weight, "tm", axis=2, tiled=True),
-        lax.all_gather(down_weight, "tm", axis=1, tiled=True),
+        define_things(down_weight),
     )
     scaled_queries = queries[0] * jnp.asarray(score_scale, jnp.bfloat16)
     offsets = jnp.where(

time: 220 us -> 248 us (1.13)
  waiting for transfers between devices: 136 us -> 157 us
  starting transfers between devices: 31.3 us -> 35.8 us
    all_gather x1, waiting for transfers between devices: 0.02 us -> 43.9 us  [on_device(): lax.all_gather(up_weight, 'tm', axis=2, tiled=True)]
    all_gather x1 -> x0, waiting for transfers between devices: 43 us -> none  [on_device(): lax.all_gather(down_weight, 'tm', axis=1, tiled=True)]
    all_to_all x0 -> x1, waiting for transfers between devices: none -> 22.3 us  [layers_all_point(): lax.all_to_all(part_next, concat_axis=0, split_axis=0, axis_name=device_a...]
    all_to_all x0 -> x1, starting transfers between devices: none -> 4.6 us  [layers_all_point(): lax.all_to_all(part_next, concat_axis=0, split_axis=0, axis_name=device_a...]
  transfers between devices with their start and end apart: 6 -> 6, of which waited for: 5 -> 6; matrix products, arithmetic and copies ran while one was open for 9% -> 3% of each run, Pallas kernels for 0% -> 0%
where the time goes in v1:
time: 248 us; the launch traced here: 247 us
  waiting for transfers between devices  157 us (63%)
  starting transfers between devices  35.8 us (14%)
  matrix products  17 us (7%)
  local copies, waits for them, and re-layouts  14.8 us (6%)
  between operations  13.7 us (6%)
  other arithmetic  8.3 us (3%)
    all_to_all x1, waiting for transfers between devices, on_device(): lax.all_to_all(produced, 'expert', split_axis=1, concat_axis=1, tiled=True)  55.9 us
    all_gather x1, waiting for transfers between devices, on_device(): lax.all_gather(up_weight, 'tm', axis=2, tiled=True)  43.9 us
    all_to_all x1, waiting for transfers between devices, layers_all_point(): lax.all_to_all(part_next, concat_axis=0, split_axis=0, axis_name=device_a...  22.3 us
    all_to_all x1, starting transfers between devices, on_device(): lax.all_to_all(slots, 'expert', split_axis=1, concat_axis=1, tiled=True)  17.6 us
    all_to_all x1, waiting for transfers between devices, on_device(): lax.all_to_all(packed, 'tm', split_axis=0, concat_axis=0, tiled=True)  16.4 us
    all_to_all x1, waiting for transfers between devices, on_device(): lax.all_to_all(slots, 'expert', split_axis=1, concat_axis=1, tiled=True)  11.3 us
    all_to_all x1, waiting for transfers between devices, on_device(): lax.all_to_all(head_out, 'tm', split_axis=0, concat_axis=0, tiled=True)  6.94 us
    dot_general x1, matrix products, on_device(): jnp.einsum('csef,efd->csed', hidden, full_down, preferred_element_type=jn...  6.22 us
  transfers between devices with their start and end apart: 6, of which 6 were waited for; matrix products, arithmetic and copies ran while one was open for 3% of the time, Pallas kernels for 0%

profile of v1, /device:TPU:32, one launch (start us, length us, event | category | flops | bytes accessed | tf_op | source)
XLA Modules:
  0.0 247.1 jit_solution(16946836829553721731)
XLA Ops:
  6.5 1.3 copy.26
  7.9 1.1 copy.27
  9.0 1.1 copy.28
  11.5 1.2 fusion.60
  12.7 5.6 %all-to-all-start = ((bf16[16,128,256]{1,2,0:T(8,128)(2,1)}), bf16[16,128,256]{1,2,0:T(8,128)(2,1)}, u32[]{:S(2)}, u32[]{:S(2)}) async-start(bf16[16,128,256]{1,2,0:T(8,128)(2,1)} %fusion.60), calls=%async_computation | async-start | bytes 2097152 | tf_op jit(solution)/shard_map/all_to_all | solution.py:86
  18.5 16.4 %all-to-all-done = bf16[16,128,256]{1,2,0:T(8,128)(2,1)} async-done(((bf16[16,128,256]{1,2,0:T(8,128)(2,1)}), bf16[16,128,256]{1,2,0:T(8,128)(2,1)}, u32[]{:S(2)}, u32[]{:S(2)}) %all-to-all-start) | async-done | bytes 1048608 | tf_op jit(solution)/shard_map/all_to_all | solution.py:86
  34.9 1.5 copy.29
  39.2 2.1 fusion
  42.3 2.5 %fusion.2 = (f32[512]{0:T(512)S(1)}, f32[512]{0:T(512)S(1)}, f32[512]{0:T(512)S(1)}) fusion(f32[512,2048]{1,0:T(8,128)S(1)} %get-tuple-element.30, f32[512]{0:T(512)S(1)} %get-tuple-element.18, f32[2048]{0:T(1024)S(1)} %convert_reduce_fusion, f32[512]{0:T(512)S(1)} %get-tuple-element.19, f32[512,2048]{1,0:T(8,128)S(1)} %fusion.73, ...), kind=kLoop, calls=%fused_computation.10 | loop fusion | flops 9435648 | bytes 12603392 | tf_op jit(solution)/shard_map/reduce_sum | solution.py:30
  48.5 3.5 %all-to-all-start.1 = ((bf16[16,128,64]{1,2,0:T(8,128)(2,1)}), bf16[16,128,64]{1,2,0:T(8,128)(2,1)S(1)}, u32[]{:S(2)}, u32[]{:S(2)}) async-start(bf16[16,128,64]{1,2,0:T(8,128)(2,1)} %copy_bitcast_fusion), calls=%async_computation.1 | async-start | bytes 524288 | tf_op jit(solution)/shard_map/all_to_all | solution.py:95
  53.1 6.9 %all-to-all-done.1 = bf16[16,128,64]{1,2,0:T(8,128)(2,1)S(1)} async-done(((bf16[16,128,64]{1,2,0:T(8,128)(2,1)}), bf16[16,128,64]{1,2,0:T(8,128)(2,1)S(1)}, u32[]{:S(2)}, u32[]{:S(2)}) %all-to-all-start.1) | async-done | bytes 262176 | tf_op jit(solution)/shard_map/all_to_all | solution.py:95
  60.0 1.6 stack.2
  61.6 4.6 %all-to-all-start.3 = ((bf16[16,1,64,1024]{3,2,1,0:T(8,128)(2,1)}), bf16[16,1,64,1024]{3,2,1,0:T(8,128)(2,1)}, u32[]{:S(2)}, u32[]{:S(2)}) async-start(bf16[16,1,64,1024]{3,2,1,0:T(8,128)(2,1)} %stack.2), calls=%async_computation.3 | async-start | bytes 4194304 | tf_op jit(solution)/shard_map/all_to_all | solution.py:14
  68.5 1.5 convolution_convert_fusion.1
  70.0 1.6 copy.34
  71.6 22.3 %all-to-all-done.3 = bf16[16,1,64,1024]{3,2,1,0:T(8,128)(2,1)} async-done(((bf16[16,1,64,1024]{3,2,1,0:T(8,128)(2,1)}), bf16[16,1,64,1024]{3,2,1,0:T(8,128)(2,1)}, u32[]{:S(2)}, u32[]{:S(2)}) %all-to-all-start.3) | async-done | bytes 2097184 | tf_op jit(solution)/shard_map/all_to_all | solution.py:14
  93.9 17.6 %all-to-all-start.2 = ((bf16[16,32,1024]{2,0,1:T(8,128)(2,1)}), bf16[16,32,1024]{2,0,1:T(8,128)(2,1)}, u32[]{:S(2)}, u32[]{:S(2)}) async-start(bf16[16,32,1024]{2,0,1:T(8,128)(2,1)} %copy.34), calls=%async_computation.2 | async-start | bytes 2097152 | tf_op jit(solution)/shard_map/all_to_all | solution.py:122
  112.2 43.9 %all-gather.2.cloned.1.call-done = bf16[1,1024,1024]{1,2,0:T(8,128)(2,1)} async-done(((bf16[1,1024,64]{1,2,0:T(8,128)(2,1)}), bf16[1,1024,1024]{1,2,0:T(8,128)(2,1)}) %all-gather.2.cloned.1.call-update) | async-done | bytes 2097168 | tf_op jit(solution)/shard_map/all_gather | solution.py:66
  156.2 11.3 %all-to-all-done.2 = bf16[16,32,1024]{2,0,1:T(8,128)(2,1)} async-done(((bf16[16,32,1024]{2,0,1:T(8,128)(2,1)}), bf16[16,32,1024]{2,0,1:T(8,128)(2,1)}, u32[]{:S(2)}, u32[]{:S(2)}) %all-to-all-start.2) | async-done | bytes 1048608 | tf_op jit(solution)/shard_map/all_to_all | solution.py:122
  167.5 6.2 %convolution_convert_fusion = bf16[16,32,1024]{2,1,0:T(8,128)(2,1)} fusion(bf16[1024,1024,1]{1,0,2:T(8,128)(2,1)} %bitcast.26, bf16[1,1024,1024]{1,2,0:T(8,128)(2,1)} %all-gather.2.cloned.1.call-done, bf16[16,32,1024]{2,0,1:T(8,128)(2,1)} %all-to-all-done.2), kind=kOutput, calls=%fused_computation.33 | convolution fusion | flops 2152726528 | bytes 6291456 | tf_op jit(solution)/shard_map/csef,efd->csed/dot_general | solution.py:129
  173.7 2.8 %copy.37 = bf16[16,32,1024]{2,0,1:T(8,128)(2,1)} copy(bf16[16,32,1024]{2,1,0:T(8,128)(2,1)} %convolution_convert_fusion) | data formatting | bytes 2097152 | tf_op jit(solution)/shard_map/convert_element_type | solution.py:131
  176.5 4.5 %all-to-all-start.4 = ((bf16[16,32,1024]{2,0,1:T(8,128)(2,1)}), bf16[16,32,1024]{2,0,1:T(8,128)(2,1)}, u32[]{:S(2)}, u32[]{:S(2)}) async-start(bf16[16,32,1024]{2,0,1:T(8,128)(2,1)} %copy.37), calls=%async_computation.4 | async-start | bytes 2097152 | tf_op jit(solution)/shard_map/all_to_all | solution.py:133
  181.3 55.9 %all-to-all-done.4 = bf16[16,32,1024]{2,0,1:T(8,128)(2,1)} async-done(((bf16[16,32,1024]{2,0,1:T(8,128)(2,1)}), bf16[16,32,1024]{2,0,1:T(8,128)(2,1)}, u32[]{:S(2)}, u32[]{:S(2)}) %all-to-all-start.4) | async-done | bytes 1048608 | tf_op jit(solution)/shard_map/all_to_all | solution.py:133
  237.2 1.8 copy.38
  (51 shorter events, 14.7 us)
Async XLA Ops:
  6.5 59.7 %copy-start = (bf16[1024,1024]{1,0:T(8,128)(2,1)S(1)}, bf16[1024,1024]{1,0:T(8,128)(2,1)}, u32[]{:S(2)}) copy-start(bf16[1024,1024]{1,0:T(8,128)(2,1)} %param.21) | copy-start | bytes 6291460
  6.5 11.7 %copy-start.5 = (s32[1,128,2]{1,2,0:T(2,128)S(1)}, s32[1,128,2]{1,2,0:T(2,128)}, u32[]{:S(2)}) copy-start(s32[1,128,2]{1,2,0:T(2,128)} %param.24) | copy-start | bytes 3076
  12.7 22.2 %all-to-all-start = ((bf16[16,128,256]{1,2,0:T(8,128)(2,1)}), bf16[16,128,256]{1,2,0:T(8,128)(2,1)}, u32[]{:S(2)}, u32[]{:S(2)}) async-start(bf16[16,128,256]{1,2,0:T(8,128)(2,1)} %fusion.60), calls=%async_computation | async-start | bytes 2097152 | tf_op jit(solution)/shard_map/all_to_all | solution.py:86
  46.7 13.3 %copy-start.2 = (bf16[1,64,1024]{2,1,0:T(8,128)(2,1)S(1)}, bf16[1,64,1024]{2,1,0:T(8,128)(2,1)}, u32[]{:S(2)}) copy-start(bf16[1,64,1024]{2,1,0:T(8,128)(2,1)} %param.27) | copy-start | bytes 393220
  47.7 18.6 %copy-start.3 = (f32[1,2,1024]{2,1,0:T(2,128)S(1)}, f32[1,2,1024]{2,1,0:T(2,128)}, u32[]{:S(2)}) copy-start(f32[1,2,1024]{2,1,0:T(2,128)} %param.23) | copy-start | bytes 24580
  47.7 18.6 %copy-start.4 = (f32[1,2,1024]{2,1,0:T(2,128)S(1)}, f32[1,2,1024]{2,1,0:T(2,128)}, u32[]{:S(2)}) copy-start(f32[1,2,1024]{2,1,0:T(2,128)} %param.22) | copy-start | bytes 24580
  47.7 18.6 %copy-start.1 = (bf16[1,128,1024]{2,1,0:T(8,128)(2,1)S(1)}, bf16[1,128,1024]{2,1,0:T(8,128)(2,1)}, u32[]{:S(2)}) copy-start(bf16[1,128,1024]{2,1,0:T(8,128)(2,1)} %param.15) | copy-start | bytes 786436
  48.5 11.6 %all-to-all-start.1 = ((bf16[16,128,64]{1,2,0:T(8,128)(2,1)}), bf16[16,128,64]{1,2,0:T(8,128)(2,1)S(1)}, u32[]{:S(2)}, u32[]{:S(2)}) async-start(bf16[16,128,64]{1,2,0:T(8,128)(2,1)} %copy_bitcast_fusion), calls=%async_computation.1 | async-start | bytes 524288 | tf_op jit(solution)/shard_map/all_to_all | solution.py:95
  61.6 32.3 %all-to-all-start.3 = ((bf16[16,1,64,1024]{3,2,1,0:T(8,128)(2,1)}), bf16[16,1,64,1024]{3,2,1,0:T(8,128)(2,1)}, u32[]{:S(2)}, u32[]{:S(2)}) async-start(bf16[16,1,64,1024]{3,2,1,0:T(8,128)(2,1)} %stack.2), calls=%async_computation.3 | async-start | bytes 4194304 | tf_op jit(solution)/shard_map/all_to_all | solution.py:14
  93.9 73.6 %all-to-all-start.2 = ((bf16[16,32,1024]{2,0,1:T(8,128)(2,1)}), bf16[16,32,1024]{2,0,1:T(8,128)(2,1)}, u32[]{:S(2)}, u32[]{:S(2)}) async-start(bf16[16,32,1024]{2,0,1:T(8,128)(2,1)} %copy.34), calls=%async_computation.2 | async-start | bytes 2097152 | tf_op jit(solution)/shard_map/all_to_all | solution.py:122
  111.5 44.7 %all-gather.2.cloned.1.call-start = ((), (), s32[]{:S(2)}) async-start(), calls=%async_computation.5 | async-start | bytes 2228224 | tf_op jit(solution)/shard_map/all_gather | solution.py:66
  173.7 65.3 %copy-start.6 = (f32[1,128,2]{1,2,0:T(2,128)S(1)}, f32[1,128,2]{1,2,0:T(2,128)}, u32[]{:S(2)}) copy-start(f32[1,128,2]{1,2,0:T(2,128)} %param.25) | copy-start | bytes 3076
  176.5 60.6 %all-to-all-start.4 = ((bf16[16,32,1024]{2,0,1:T(8,128)(2,1)}), bf16[16,32,1024]{2,0,1:T(8,128)(2,1)}, u32[]{:S(2)}, u32[]{:S(2)}) async-start(bf16[16,32,1024]{2,0,1:T(8,128)(2,1)} %copy.37), calls=%async_computation.4 | async-start | bytes 2097152 | tf_op jit(solution)/shard_map/all_to_all | solution.py:133
Sparse Core Ops, SparseCore 0:
  114.5 41.6 all-gather.1
